TPU v7x, 128 devices: a whole 4x4x4 slice. The times are simulated.
128 devices in a mesh: row: 8 (over y_hi, x), col: 16 (over z, y_lo, core).
Axes of the slice: x: 4, y: 4 (y_hi: 2, y_lo: 2; y = y_hi * 2 + y_lo), z: 4, core: 2. Of those that a mesh axis runs over, the one named last changes fastest.
Arguments:
- features: bfloat16 [64, 1024, 1024], P(None, 'col', 'row'), may hold values from -120 to 120
- conv_first: bfloat16 [9, 64, 64], replicated, may hold values from -0.25 to 0.25
- conv_second: bfloat16 [9, 64, 64], replicated, may hold values from -0.25 to 0.25
- head_weight: bfloat16 [37, 64], replicated, may hold values from -0.75 to 0.75
- head_bias: float32 [37], replicated, may hold values from -4 to 4
- cotangent: bfloat16 [37, 1024, 1024], P(None, 'col', 'row'), may hold values from -6 to 6
Outputs:
- logits: bfloat16 [37, 1024, 1024], P(None, 'col', 'row')
- input_grad: bfloat16 [64, 1024, 1024], P(None, 'col', 'row')
- grad_first: float32 [9, 64, 64], replicated
- grad_second: float32 [9, 64, 64], replicated
- grad_head: float32 [37, 64], replicated
- grad_bias: float32 [37], replicated
All inputs are finite; a program needn't handle non-finite values.
Results may differ from a plain program's by a relative error of at most 0.007.
Values may be sent and summed in bfloat16 or wider, within the bound.
No kernel may reach another device: no remote copies, remote signals or barrier semaphores. Data moves between devices by JAX's collectives and lax.ppermute only.
A program may use at most 128 MiB of HBM per device.

v0:
```python
import jax
import jax.numpy as jnp
from jax import lax
from jax.sharding import PartitionSpec as P

DILATION_STEP = 16
epsilon = 1e-05


def with_halo(block, sides, width):
    for axis, dim in sides:
        count = lax.axis_size(axis)
        forward = [(i, i + 1) for i in range(count - 1)]
        backward = [(target, source) for source, target in forward]
        low = lax.ppermute(
            lax.slice_in_dim(block, block.shape[dim] - width, None, axis=dim), axis, forward
        )
        high = lax.ppermute(lax.slice_in_dim(block, 0, width, axis=dim), axis, backward)
        block = jnp.concatenate([low, block, high], axis=dim)
    return block


def as_sent(shard):

    def short(part):
        return part.astype(jnp.bfloat16) if part.dtype == jnp.float32 else part

    return jax.tree.map(short, shard)


def elu_apply(value_entries):
    return jnp.where(
        value_entries > 0, value_entries, jnp.exp(jnp.minimum(value_entries, 0.0)) - 1.0
    )


def elu_slope(value_entries):
    return jnp.where(value_entries > 0, 1.0, jnp.exp(jnp.minimum(value_entries, 0.0)))


def widen(value_entries):
    return with_halo(value_entries, (("row", 2), ("col", 1)), DILATION_STEP)


def widen_grad(value_entries):
    return with_halo(value_entries, (("row", 2), ("col", 1)), DILATION_STEP)


def tap_window(padded, kernel_row, kernel_column, adjoint, col_count, row_count):
    shift_direction = -1 if adjoint else 1
    column_shift = DILATION_STEP + shift_direction * DILATION_STEP * (kernel_column - 1)
    row_shift = DILATION_STEP + shift_direction * DILATION_STEP * (kernel_row - 1)
    window = padded[:, column_shift : column_shift + col_count, row_shift : row_shift + row_count]
    return window.reshape(padded.shape[0], col_count * row_count)


def convolve(padded, weights, col_count, row_count, adjoint):
    running = jnp.zeros((weights.shape[1], col_count * row_count), jnp.float32)
    for kernel_row in range(3):
        for kernel_column in range(3):
            window = tap_window(padded, kernel_row, kernel_column, adjoint, col_count, row_count)
            matrix = weights[3 * kernel_row + kernel_column]
            if adjoint:
                matrix = matrix.T
            running = running + jnp.dot(matrix, window, preferred_element_type=jnp.float32)
    return running.reshape(-1, col_count, row_count)


def weight_terms(gradient, padded, col_count, row_count):
    flattened = gradient.reshape(gradient.shape[0], -1)
    collected = []
    for kernel_row in range(3):
        for kernel_column in range(3):
            window = tap_window(padded, kernel_row, kernel_column, False, col_count, row_count)
            collected.append(
                lax.dot_general(
                    flattened, window, (((1,), (1,)), ((), ())), preferred_element_type=jnp.float32
                )
            )
    return jnp.stack(collected, 0)


def normalize(activation, cell_count):
    totals = lax.psum(jnp.sum(activation, axis=(1, 2)), ("row", "col"))
    average = totals / cell_count
    centered = activation - average[:, None, None]
    spread = lax.psum(jnp.sum(centered * centered, axis=(1, 2)), ("row", "col")) / cell_count
    inverse_std = lax.rsqrt(spread + epsilon)
    return (centered * inverse_std[:, None, None], inverse_std)


def norm_back(gradient, normed, inverse_std, cell_count):
    first_sum, second_sum = lax.psum(
        (jnp.sum(gradient, axis=(1, 2)), jnp.sum(gradient * normed, axis=(1, 2))), ("row", "col")
    )
    first_mean = first_sum / cell_count
    second_mean = second_sum / cell_count
    return inverse_std[:, None, None] * (
        gradient - first_mean[:, None, None] - normed * second_mean[:, None, None]
    )


def mirror_prepare(tensor, col_devices):
    planes, col_count, row_count = tensor.shape
    slab_rows = row_count // col_devices
    shaped = tensor.reshape(planes, col_count, col_devices, slab_rows).transpose(2, 1, 0, 3)
    return shaped.reshape(col_devices, col_count, planes * slab_rows)


def mirror_middle(received):
    return received.reshape(received.shape[1], 1, received.shape[2])


def mirror_tail(received, col_devices, row_devices):
    return received.reshape(received.shape[0], col_devices, row_devices, received.shape[2])


def mirror_finish(received, planes, row_devices):
    row_count = received.shape[0]
    slab_rows = received.shape[3] // planes
    shaped = received.reshape(row_count, row_devices, planes, slab_rows).transpose(2, 1, 3, 0)
    return shaped.reshape(planes, row_devices * slab_rows, row_count)


def mirror_half(tensors):
    col_devices = lax.axis_size("col")
    row_devices = lax.axis_size("row")
    planes = tuple((member.shape[0] for member in tensors))
    first = lax.all_to_all(
        as_sent(tuple((mirror_prepare(member, col_devices) for member in tensors))),
        "col",
        split_axis=0,
        concat_axis=1,
        tiled=True,
    )
    second = lax.all_to_all(
        as_sent(tuple((mirror_middle(member) for member in first))),
        ("row", "col"),
        split_axis=0,
        concat_axis=1,
        tiled=True,
    )
    third = lax.all_to_all(
        as_sent(tuple((mirror_tail(member, col_devices, row_devices) for member in second))),
        "col",
        split_axis=1,
        concat_axis=0,
        tiled=True,
    )
    return tuple(
        (
            mirror_finish(member, count_planes, row_devices)
            for member, count_planes in zip(third, planes)
        )
    )


def mirror_full(tensors):
    col_devices = lax.axis_size("col")
    row_devices = lax.axis_size("row")
    planes = tuple((member.shape[0] for member in tensors))
    first = lax.all_to_all(
        tuple((mirror_prepare(member, col_devices) for member in tensors)),
        "col",
        split_axis=0,
        concat_axis=1,
        tiled=True,
    )
    second = lax.all_to_all(
        tuple((mirror_middle(member) for member in first)),
        ("row", "col"),
        split_axis=0,
        concat_axis=1,
        tiled=True,
    )
    third = lax.all_to_all(
        tuple((mirror_tail(member, col_devices, row_devices) for member in second)),
        "col",
        split_axis=1,
        concat_axis=0,
        tiled=True,
    )
    return tuple(
        (
            mirror_finish(member, count_planes, row_devices)
            for member, count_planes in zip(third, planes)
        )
    )


def on_device(features, conv_first, conv_second, head_weight, head_bias, cotangent):
    channels, col_count, row_count = features.shape
    length = col_count * lax.axis_size("col")
    cell_count = float(length * length)
    cot_mirror = mirror_half((cotangent,))[0]
    wide_in = widen(features)
    act_first = convolve(wide_in, conv_first, col_count, row_count, False)
    normed_first, inverse_first = normalize(act_first, cell_count)
    hidden_first = elu_apply(normed_first).astype(jnp.bfloat16)
    wide_hidden = widen(hidden_first)
    act_second = convolve(wide_hidden, conv_second, col_count, row_count, False)
    normed_second, inverse_second = normalize(act_second, cell_count)
    summed = normed_second + features.astype(jnp.float32)
    hidden = elu_apply(summed).astype(jnp.bfloat16)
    flat_hidden = hidden.reshape(channels, -1)
    raw_logits = (
        jnp.dot(head_weight, flat_hidden, preferred_element_type=jnp.float32) + head_bias[:, None]
    ).reshape(-1, col_count, row_count)
    logit_mirror = mirror_full((raw_logits,))[0]
    logits = (0.5 * (raw_logits + logit_mirror)).astype(jnp.bfloat16)
    grad_sym = (0.5 * (cotangent.astype(jnp.float32) + cot_mirror.astype(jnp.float32))).astype(
        jnp.bfloat16
    )
    flat_sym = grad_sym.reshape(grad_sym.shape[0], -1)
    bias_term = jnp.sum(flat_sym, axis=1, dtype=jnp.float32)
    head_term = lax.dot_general(
        flat_sym, flat_hidden, (((1,), (1,)), ((), ())), preferred_element_type=jnp.float32
    )
    grad_hidden = jnp.dot(head_weight.T, flat_sym, preferred_element_type=jnp.float32).reshape(
        channels, col_count, row_count
    )
    grad_summed = grad_hidden * elu_slope(summed)
    grad_act_second = norm_back(grad_summed, normed_second, inverse_second, cell_count).astype(
        jnp.bfloat16
    )
    second_term = weight_terms(grad_act_second, wide_hidden, col_count, row_count)
    grad_hidden_first = convolve(
        widen_grad(grad_act_second), conv_second, col_count, row_count, True
    )
    grad_normed_first = grad_hidden_first * elu_slope(normed_first)
    grad_act_first = norm_back(grad_normed_first, normed_first, inverse_first, cell_count).astype(
        jnp.bfloat16
    )
    first_term = weight_terms(grad_act_first, wide_in, col_count, row_count)
    input_grad = (
        convolve(widen_grad(grad_act_first), conv_first, col_count, row_count, True) + grad_summed
    ).astype(jnp.bfloat16)
    reduced = lax.psum((first_term, second_term, head_term, bias_term), ("row", "col"))
    inverse_len = 1.0 / length
    return (
        logits,
        input_grad,
        reduced[0] * inverse_len,
        reduced[1] * inverse_len,
        reduced[2] * inverse_len,
        reduced[3] * inverse_len,
    )


def solution(mesh):
    placed = (P(None, "col", "row"), P(), P(), P(), P(), P(None, "col", "row"))
    return jax.shard_map(
        on_device,
        mesh=mesh,
        in_specs=placed,
        out_specs=(P(None, "col", "row"), P(None, "col", "row"), P(), P(), P(), P()),
        check_vma=False,
    )
```

profile of v0, /device:TPU:1, one launch (start us, length us, event | category | flops | bytes accessed | tf_op | source)
XLA Modules:
  0.0 945.5 jit_solution(8504347659862040630)
XLA Ops:
  12.6 5.3 collective-permute-start
  21.0 7.8 all-to-all-start.3
  45.4 7.2 collective-permute-done.3
  63.5 67.2 %psum.84 = f32[64]{0:T(128)S(1)} all-reduce(f32[64]{0:T(128)S(1)} %get-tuple-element.108), channel_id=1, replica_groups=mesh['row'=8,'col'=16] {'row','col'}, use_global_device_ids=true, to_apply=%region_1.0 | all-reduce | flops 64 | bytes 512 | tf_op jit(solution)/shard_map/psum | solution.py:84
  131.1 63.5 %psum.85 = f32[64]{0:T(128)S(1)} all-reduce(f32[64]{0:T(128)S(1)} %multiply_reduce_fusion.2), channel_id=1, replica_groups=mesh['row'=8,'col'=16] {'row','col'}, use_global_device_ids=true, to_apply=%region_3.0 | all-reduce | flops 64 | bytes 512 | tf_op jit(solution)/shard_map/psum | solution.py:87
  233.1 11.2 %all-to-all-start.4 = ((bf16[128,2,1184]{2,1,0:T(2,128)(2,1)}), bf16[128,2,1184]{2,1,0:T(2,128)(2,1)}, u32[]{:S(2)}, u32[]{:S(2)}) async-start(bf16[128,2,1184]{2,1,0:T(2,128)(2,1)} %reshape.289), calls=%async_computation.4 | async-start | bytes 1310720 | tf_op jit(solution)/shard_map/all_to_all | solution.py:136
  260.6 67.2 %psum.86 = f32[64]{0:T(128)S(1)} all-reduce(f32[64]{0:T(128)S(1)} %get-tuple-element.110), channel_id=1, replica_groups=mesh['row'=8,'col'=16] {'row','col'}, use_global_device_ids=true, to_apply=%region_5.6 | all-reduce | flops 64 | bytes 512 | tf_op jit(solution)/shard_map/psum | solution.py:84
  327.7 6.2 reshape.290
  342.8 65.3 %psum.87 = f32[64]{0:T(128)S(1)} all-reduce(f32[64]{0:T(128)S(1)} %fusion.19), channel_id=1, replica_groups=mesh['row'=8,'col'=16] {'row','col'}, use_global_device_ids=true, to_apply=%region_7.8 | all-reduce | flops 64 | bytes 512 | tf_op jit(solution)/shard_map/psum | solution.py:87
  409.4 12.2 %reshape.288 = f32[128,8,37,8]{3,2,1,0:T(8,128)} reshape(f32[16,8,1,8,296]{4,3,1,0,2:T(8,128)} %convert_bitcast_fusion) | data formatting | bytes 2424832 | tf_op jit(solution)/shard_map/convert_element_type | solution.py:211
  421.5 11.1 %copy.273 = f32[37,8,8,128]{3,2,1,0:T(8,128)S(1)} copy(f32[37,8,8,128]{2,0,1,3:T(8,128)} %bitcast.528) | data formatting | bytes 2424832 | tf_op jit(solution)/shard_map/convert_element_type | solution.py:211
  439.4 62.9 %all-reduce.1 = (f32[64]{0:T(128)S(1)}, f32[64]{0:T(128)S(1)}) all-reduce(f32[64]{0:T(128)S(1)} %get-tuple-element.39, f32[64]{0:T(128)S(1)} %get-tuple-element.38), channel_id=1, replica_groups=mesh['row'=8,'col'=16] {'row','col'}, use_global_device_ids=true, to_apply=%region_11.12 | all-reduce | flops 128 | bytes 1024 | tf_op jit(solution)/shard_map/psum | solution.py:93
  538.7 5.1 copy.259
  546.9 5.3 all-to-all-start
  568.5 8.1 collective-permute-done.11
  576.5 7.2 collective-permute-done.10
  595.0 67.2 %all-reduce = (f32[64]{0:T(128)S(1)}, f32[64]{0:T(128)S(1)}, f32[37,64]{1,0:T(8,128)S(1)}, f32[37]{0:T(128)S(1)}) all-reduce(f32[64]{0:T(128)S(1)} %get-tuple-element.37, f32[64]{0:T(128)S(1)} %get-tuple-element.36, f32[37,64]{1,0:T(8,128)S(1)} %convolution_bitcast_fusion.23, ...), channel_id=1, replica_groups=mesh['row'=8,'col'=16] {'row','col'}, use_global_device_ids=true, to_apply=%region_15.16 | all-reduce | flops 2533 | bytes 20264 | tf_op jit(solution)/shard_map/psum | solution.py:93
  708.2 125.5 %all-reduce.5.cloned.1.call-done = (f32[9,64,64]{2,1,0:T(8,128)}, f32[9,64,64]{2,1,0:T(8,128)}) async-done(((f32[9,64,64]{2,1,0:T(8,128)}, f32[9,64,64]{2,1,0:T(8,128)}), (f32[9,64,64]{2,1,0:T(8,128)}, f32[9,64,64]{2,1,0:T(8,128)})) %all-reduce.5.cloned.1.call-update) | async-done | bytes 294928 | tf_op jit(solution)/shard_map/psum | solution.py:238
  852.7 7.4 all-to-all-start.1
  866.1 17.9 %all-to-all-done.1 = f32[1024,1,296]{2,1,0:T(1,128)} async-done(((f32[1024,1,296]{2,1,0:T(1,128)}), f32[1024,1,296]{2,1,0:T(1,128)}, u32[]{:S(2)}, u32[]{:S(2)}) %all-to-all-start.1) | async-done | bytes 1212448 | tf_op jit(solution)/shard_map/all_to_all | solution.py:169
  887.0 5.5 all-to-all-start.2
  898.6 15.5 %all-to-all-done.2 = f32[8,16,8,296]{3,2,0,1:T(8,128)} async-done(((f32[8,16,8,296]{3,2,0,1:T(8,128)}), f32[8,16,8,296]{3,2,0,1:T(8,128)}, u32[]{:S(2)}, u32[]{:S(2)}) %all-to-all-start.2) | async-done | bytes 1212448 | tf_op jit(solution)/shard_map/all_to_all | solution.py:176
  914.1 12.2 %reshape.287 = f32[128,8,37,8]{3,2,1,0:T(8,128)} reshape(f32[16,8,1,8,296]{4,3,1,0,2:T(8,128)} %bitcast.32) | data formatting | bytes 2424832 | tf_op jit(solution)/shard_map/reshape | solution.py:121
  926.2 11.2 %copy.265 = f32[37,8,8,128]{3,2,1,0:T(8,128)S(1)} copy(f32[37,8,8,128]{2,0,1,3:T(8,128)} %bitcast.529) | data formatting | bytes 2424832 | tf_op jit(solution)/shard_map/transpose | solution.py:121
  (269 shorter events, 255.1 us)
Async XLA Ops:
  7.2 427.7 %copy-start = (bf16[37,64]{1,0:T(8,128)(2,1)S(1)}, bf16[37,64]{1,0:T(8,128)(2,1)}, u32[]{:S(2)}) copy-start(bf16[37,64]{1,0:T(8,128)(2,1)} %param.9) | copy-start | bytes 14212
  10.3 22.0 %collective-permute-start.1 = (bf16[64,64,16]{1,2,0:T(8,128)(2,1)}, bf16[64,64,16]{1,2,0:T(8,128)(2,1)}, u32[]{:S(2)}, u32[]{:S(2)}) collective-permute-start(bf16[64,64,16]{1,2,0:T(8,128)(2,1)} %copy.320), channel_id=1, source_target_pairs={{16,0},{32,16},{48,32},{64,48},{80,64},{96,80},{112,96},{17,1},{33... | collective-permute-start | bytes 393224 | tf_op jit(solution)/shard_map/ppermute | solution.py:18
  12.6 16.9 %collective-permute-start = (bf16[64,64,16]{1,2,0:T(8,128)(2,1)}, bf16[64,64,16]{1,2,0:T(8,128)(2,1)}, u32[]{:S(2)}, u32[]{:S(2)}) collective-permute-start(bf16[64,64,16]{1,2,0:T(8,128)(2,1)} %copy.319), channel_id=1, source_target_pairs={{0,16},{16,32},{32,48},{48,64},{64,80},{80,96},{96,112},{1,17},{17... | collective-permute-start | bytes 393224 | tf_op jit(solution)/shard_map/ppermute | solution.py:15
  21.0 205.0 %all-to-all-start.3 = ((bf16[16,64,296]{2,1,0:T(8,128)(2,1)}), bf16[16,64,296]{2,1,0:T(8,128)(2,1)}, u32[]{:S(2)}, u32[]{:S(2)}) async-start(bf16[16,64,296]{2,1,0:T(8,128)(2,1)} %copy.268), calls=%async_computation.3 | async-start | bytes 1572864 | tf_op jit(solution)/shard_map/all_to_all | solution.py:129
  35.7 9.7 %collective-permute-start.2 = (bf16[64,16,160]{2,0,1:T(8,128)(2,1)S(1)}, bf16[64,16,160]{2,0,1:T(8,128)(2,1)S(1)}, u32[]{:S(2)}, u32[]{:S(2)}) collective-permute-start(bf16[64,16,160]{2,0,1:T(8,128)(2,1)S(1)} %get-tuple-element.66), channel_id=1, source_target_pairs={{0,1},{1,2},{2,3},{3,4},{4,5},{5,6},{6,7},{7,8},{8,9},{9,10},{10,1... | collective-permute-start | bytes 983048 | tf_op jit(solution)/shard_map/ppermute | solution.py:15
  39.3 13.3 %collective-permute-start.3 = (bf16[64,16,160]{2,0,1:T(8,128)(2,1)S(1)}, bf16[64,16,160]{2,0,1:T(8,128)(2,1)S(1)}, u32[]{:S(2)}, u32[]{:S(2)}) collective-permute-start(bf16[64,16,160]{2,0,1:T(8,128)(2,1)S(1)} %get-tuple-element.67), channel_id=1, source_target_pairs={{1,0},{2,1},{3,2},{4,3},{5,4},{6,5},{7,6},{8,7},{9,8},{10,9},{11,1... | collective-permute-start | bytes 983048 | tf_op jit(solution)/shard_map/ppermute | solution.py:18
  199.3 7.2 collective-permute-start.4
  205.2 8.9 collective-permute-start.5
  220.2 27.0 %collective-permute-start.7 = (bf16[64,16,160]{2,0,1:T(8,128)(2,1)}, bf16[64,16,160]{2,0,1:T(8,128)(2,1)}, u32[]{:S(2)}, u32[]{:S(2)}) collective-permute-start(bf16[64,16,160]{2,0,1:T(8,128)(2,1)} %get-tuple-element.62), channel_id=1, source_target_pairs={{1,0},{2,1},{3,2},{4,3},{5,4},{6,5},{7,6},{8,7},{9,8},{10,9},{11,1... | collective-permute-start | bytes 983048 | tf_op jit(solution)/shard_map/ppermute | solution.py:18
  224.1 23.1 %collective-permute-start.6 = (bf16[64,16,160]{2,0,1:T(8,128)(2,1)}, bf16[64,16,160]{2,0,1:T(8,128)(2,1)}, u32[]{:S(2)}, u32[]{:S(2)}) collective-permute-start(bf16[64,16,160]{2,0,1:T(8,128)(2,1)} %get-tuple-element.63), channel_id=1, source_target_pairs={{0,1},{1,2},{2,3},{3,4},{4,5},{5,6},{6,7},{7,8},{8,9},{9,10},{10,1... | collective-permute-start | bytes 983048 | tf_op jit(solution)/shard_map/ppermute | solution.py:15
  233.1 94.7 %all-to-all-start.4 = ((bf16[128,2,1184]{2,1,0:T(2,128)(2,1)}), bf16[128,2,1184]{2,1,0:T(2,128)(2,1)}, u32[]{:S(2)}, u32[]{:S(2)}) async-start(bf16[128,2,1184]{2,1,0:T(2,128)(2,1)} %reshape.289), calls=%async_computation.4 | async-start | bytes 1310720 | tf_op jit(solution)/shard_map/all_to_all | solution.py:136
  336.5 71.6 %all-to-all-start.5 = ((bf16[8,16,8,296]{3,2,0,1:T(8,128)(2,1)}), bf16[8,16,8,296]{3,2,0,1:T(8,128)(2,1)S(1)}, u32[]{:S(2)}, u32[]{:S(2)}) async-start(bf16[8,16,8,296]{3,2,0,1:T(8,128)(2,1)} %copy.271), calls=%async_computation.5 | async-start | bytes 1572864 | tf_op jit(solution)/shard_map/all_to_all | solution.py:143
  522.8 33.1 %collective-permute-start.9 = (bf16[64,64,16]{1,2,0:T(8,128)(2,1)}, bf16[64,64,16]{1,2,0:T(8,128)(2,1)}, u32[]{:S(2)}, u32[]{:S(2)}) collective-permute-start(bf16[64,64,16]{1,2,0:T(8,128)(2,1)} %copy.276), channel_id=1, source_target_pairs={{16,0},{32,16},{48,32},{64,48},{80,64},{96,80},{112,96},{17,1},{33... | collective-permute-start | bytes 393224 | tf_op jit(solution)/shard_map/ppermute | solution.py:18
  524.1 28.4 %collective-permute-start.8 = (bf16[64,64,16]{1,2,0:T(8,128)(2,1)}, bf16[64,64,16]{1,2,0:T(8,128)(2,1)}, u32[]{:S(2)}, u32[]{:S(2)}) collective-permute-start(bf16[64,64,16]{1,2,0:T(8,128)(2,1)} %copy.275), channel_id=1, source_target_pairs={{0,16},{16,32},{32,48},{48,64},{64,80},{80,96},{96,112},{1,17},{17... | collective-permute-start | bytes 393224 | tf_op jit(solution)/shard_map/ppermute | solution.py:15
  546.9 301.6 %all-to-all-start = ((f32[16,64,296]{2,1,0:T(8,128)}), f32[16,64,296]{2,1,0:T(8,128)}, u32[]{:S(2)}, u32[]{:S(2)}) async-start(f32[16,64,296]{2,1,0:T(8,128)} %copy.260), calls=%async_computation | async-start | bytes 3145728 | tf_op jit(solution)/shard_map/all_to_all | solution.py:162
  552.3 281.4 %all-reduce.5.cloned.1.call-start = ((), (), s32[]{:S(2)}) async-start(), calls=%async_computation.6 | async-start | bytes 1179648 | tf_op jit(solution)/shard_map/psum | solution.py:238
  561.2 15.3 %collective-permute-start.11 = (bf16[64,16,160]{2,0,1:T(8,128)(2,1)S(1)}, bf16[64,16,160]{2,0,1:T(8,128)(2,1)S(1)}, u32[]{:S(2)}, u32[]{:S(2)}) collective-permute-start(bf16[64,16,160]{2,0,1:T(8,128)(2,1)S(1)} %get-tuple-element.58), channel_id=1, source_target_pairs={{0,1},{1,2},{2,3},{3,4},{4,5},{5,6},{6,7},{7,8},{8,9},{9,10},{10,1... | collective-permute-start | bytes 983048 | tf_op jit(solution)/shard_map/ppermute | solution.py:15
  564.8 18.9 %collective-permute-start.10 = (bf16[64,16,160]{2,0,1:T(8,128)(2,1)S(1)}, bf16[64,16,160]{2,0,1:T(8,128)(2,1)S(1)}, u32[]{:S(2)}, u32[]{:S(2)}) collective-permute-start(bf16[64,16,160]{2,0,1:T(8,128)(2,1)S(1)} %get-tuple-element.59), channel_id=1, source_target_pairs={{1,0},{2,1},{3,2},{4,3},{5,4},{6,5},{7,6},{8,7},{9,8},{10,9},{11,1... | collective-permute-start | bytes 983048 | tf_op jit(solution)/shard_map/ppermute | solution.py:18
  679.5 13.4 %collective-permute-start.13 = (bf16[64,64,16]{1,2,0:T(8,128)(2,1)}, bf16[64,64,16]{1,2,0:T(8,128)(2,1)}, u32[]{:S(2)}, u32[]{:S(2)}) collective-permute-start(bf16[64,64,16]{1,2,0:T(8,128)(2,1)} %copy.292), channel_id=1, source_target_pairs={{16,0},{32,16},{48,32},{64,48},{80,64},{96,80},{112,96},{17,1},{33... | collective-permute-start | bytes 393224 | tf_op jit(solution)/shard_map/ppermute | solution.py:18
  680.8 8.8 collective-permute-start.12
  699.2 137.9 %collective-permute-start.15 = (bf16[64,16,160]{2,0,1:T(8,128)(2,1)}, bf16[64,16,160]{2,0,1:T(8,128)(2,1)}, u32[]{:S(2)}, u32[]{:S(2)}) collective-permute-start(bf16[64,16,160]{2,0,1:T(8,128)(2,1)} %get-tuple-element.54), channel_id=1, source_target_pairs={{0,1},{1,2},{2,3},{3,4},{4,5},{5,6},{6,7},{7,8},{8,9},{9,10},{10,1... | collective-permute-start | bytes 983048 | tf_op jit(solution)/shard_map/ppermute | solution.py:15
  703.8 133.3 %collective-permute-start.14 = (bf16[64,16,160]{2,0,1:T(8,128)(2,1)}, bf16[64,16,160]{2,0,1:T(8,128)(2,1)}, u32[]{:S(2)}, u32[]{:S(2)}) collective-permute-start(bf16[64,16,160]{2,0,1:T(8,128)(2,1)} %get-tuple-element.55), channel_id=1, source_target_pairs={{1,0},{2,1},{3,2},{4,3},{5,4},{6,5},{7,6},{8,7},{9,8},{10,9},{11,1... | collective-permute-start | bytes 983048 | tf_op jit(solution)/shard_map/ppermute | solution.py:18
  852.7 31.3 %all-to-all-start.1 = ((f32[1024,1,296]{2,1,0:T(1,128)}), f32[1024,1,296]{2,1,0:T(1,128)}, u32[]{:S(2)}, u32[]{:S(2)}) async-start(f32[1024,1,296]{2,1,0:T(1,128)} %copy.261), calls=%async_computation.1 | async-start | bytes 3145728 | tf_op jit(solution)/shard_map/all_to_all | solution.py:169
  887.0 27.1 %all-to-all-start.2 = ((f32[8,16,8,296]{3,2,0,1:T(8,128)}), f32[8,16,8,296]{3,2,0,1:T(8,128)}, u32[]{:S(2)}, u32[]{:S(2)}) async-start(f32[8,16,8,296]{3,2,0,1:T(8,128)} %copy.263), calls=%async_computation.2 | async-start | bytes 3145728 | tf_op jit(solution)/shard_map/all_to_all | solution.py:176
  (48 other events, 293.1 us)
Sparse Core Ops, SparseCore 0:
  686.0 147.6 all-reduce.4
where the time goes:
time: 954 us; the launch traced here: 946 us
  blocking collectives  393 us (41%)
  waiting for transfers between devices  191 us (20%)
  local copies, waits for them, and re-layouts  156 us (16%)
  starting transfers between devices  88.6 us (9%)
  other arithmetic  55 us (6%)
  matrix products  46.3 us (5%)
  between operations  15.3 us (2%)
    psum x2, blocking collectives, normalize(): totals = lax.psum(jnp.sum(activation, axis=(1, 2)), ('row', 'col'))  134 us
    psum x2, blocking collectives, norm_back(): lax.psum((jnp.sum(gradient, axis=(1, 2)), jnp.sum(gradient * normed, axis...  130 us
    psum x2, blocking collectives, normalize(): lax.psum(jnp.sum(centered * centered, axis=(1, 2)), ('row', 'col'))  129 us
    psum x1, waiting for transfers between devices, on_device(): lax.psum((first_term, second_term, head_term, bias_term), ('row', 'col'))  125 us
    unnamed x117, local copies, waits for them, and re-layouts  38.8 us
    ppermute x8, starting transfers between devices, with_halo(): lax.ppermute(lax.slice_in_dim(block, block.shape[dim] - width, None, axis...  31.6 us
    dot_general x36, matrix products, convolve(): jnp.dot(matrix, window, preferred_element_type=jnp.float32)  25.6 us
    convert_element_type x2, local copies, waits for them, and re-layouts, on_device(): cot_mirror.astype(jnp.float32)  23.2 us
  transfers between devices with their start and end apart: 23, of which 9 were waited for; matrix products, arithmetic and copies ran while one was open for 16% of the time, Pallas kernels for 0%

commit v1 on v0

--- a/solution.py
+++ b/solution.py
@@ -84,7 +84,10 @@
     totals = lax.psum(jnp.sum(activation, axis=(1, 2)), ("row", "col"))
     average = totals / cell_count
     centered = activation - average[:, None, None]
-    spread = lax.psum(jnp.sum(centered * centered, axis=(1, 2)), ("row", "col")) / cell_count
+    spread = (
+        jnp.sum(lax.all_gather(jnp.sum(centered * centered, axis=(1, 2)), ("row", "col")), axis=0)
+        / cell_count
+    )
     inverse_std = lax.rsqrt(spread + epsilon)
     return (centered * inverse_std[:, None, None], inverse_std)
 

time: 954 us -> 954 us (level)
    psum x2 -> x0, blocking collectives: 129 us -> none  [normalize(): lax.psum(jnp.sum(centered * centered, axis=(1, 2)), ('row', 'col'))]
    unnamed x0 -> x2, blocking collectives: none -> 129 us
    unnamed x117 -> x121, local copies, waits for them, and re-layouts: 38.8 us -> 39.3 us
where the time goes in v1:
time: 954 us; the launch traced here: 946 us
  blocking collectives  392 us (41%)
  waiting for transfers between devices  191 us (20%)
  local copies, waits for them, and re-layouts  157 us (16%)
  starting transfers between devices  89 us (9%)
  other arithmetic  55.2 us (6%)
  matrix products  46.3 us (5%)
  between operations  15.3 us (2%)
    psum x2, blocking collectives, normalize(): totals = lax.psum(jnp.sum(activation, axis=(1, 2)), ('row', 'col'))  134 us
    psum x2, blocking collectives, norm_back(): lax.psum((jnp.sum(gradient, axis=(1, 2)), jnp.sum(gradient * normed, axis...  129 us
    unnamed x2, blocking collectives  129 us
    psum x1, waiting for transfers between devices, on_device(): lax.psum((first_term, second_term, head_term, bias_term), ('row', 'col'))  125 us
    unnamed x121, local copies, waits for them, and re-layouts  39.3 us
    ppermute x8, starting transfers between devices, with_halo(): lax.ppermute(lax.slice_in_dim(block, block.shape[dim] - width, None, axis...  31.7 us
    dot_general x36, matrix products, convolve(): jnp.dot(matrix, window, preferred_element_type=jnp.float32)  25.6 us
    convert_element_type x2, local copies, waits for them, and re-layouts, on_device(): cot_mirror.astype(jnp.float32)  23.2 us
  transfers between devices with their start and end apart: 23, of which 9 were waited for; matrix products, arithmetic and copies ran while one was open for 16% of the time, Pallas kernels for 0%

profile of v1, /device:TPU:1, one launch (start us, length us, event | category | flops | bytes accessed | tf_op | source)
XLA Modules:
  0.0 945.9 jit_solution(4472165437969287457)
XLA Ops:
  12.6 5.3 collective-permute-start
  21.1 7.8 all-to-all-start.3
  45.4 7.2 collective-permute-done.3
  63.5 67.2 %psum.70 = f32[64]{0:T(128)S(1)} all-reduce(f32[64]{0:T(128)S(1)} %get-tuple-element.108), channel_id=1, replica_groups=mesh['row'=8,'col'=16] {'row','col'}, use_global_device_ids=true, to_apply=%region_1.0 | all-reduce | flops 64 | bytes 512 | tf_op jit(solution)/shard_map/psum | solution.py:84
  131.3 63.5 %all-reduce = f32[8192]{0:T(1024)S(1)} all-reduce(f32[8192]{0:T(1024)S(1)} %dynamic-update-slice), channel_id=2, replica_groups=mesh['row'=8,'col'=16] {'row','col'}, use_global_device_ids=true, to_apply=%add | all-reduce | flops 8192 | bytes 65536
  233.5 11.3 %all-to-all-start.4 = ((bf16[128,2,1184]{2,1,0:T(2,128)(2,1)}), bf16[128,2,1184]{2,1,0:T(2,128)(2,1)}, u32[]{:S(2)}, u32[]{:S(2)}) async-start(bf16[128,2,1184]{2,1,0:T(2,128)(2,1)} %reshape.303), calls=%async_computation.4 | async-start | bytes 1310720 | tf_op jit(solution)/shard_map/all_to_all | solution.py:139
  261.2 67.2 %psum.71 = f32[64]{0:T(128)S(1)} all-reduce(f32[64]{0:T(128)S(1)} %get-tuple-element.110), channel_id=1, replica_groups=mesh['row'=8,'col'=16] {'row','col'}, use_global_device_ids=true, to_apply=%region_5.6 | all-reduce | flops 64 | bytes 512 | tf_op jit(solution)/shard_map/psum | solution.py:84
  328.4 6.2 reshape.304
  343.7 65.1 %all-reduce.1 = f32[8192]{0:T(1024)S(1)} all-reduce(f32[8192]{0:T(1024)S(1)} %dynamic-update-slice.1), channel_id=3, replica_groups=mesh['row'=8,'col'=16] {'row','col'}, use_global_device_ids=true, to_apply=%add.1 | all-reduce | flops 8192 | bytes 65536
  410.2 12.2 %reshape.302 = f32[128,8,37,8]{3,2,1,0:T(8,128)} reshape(f32[16,8,1,8,296]{4,3,1,0,2:T(8,128)} %convert_bitcast_fusion) | data formatting | bytes 2424832 | tf_op jit(solution)/shard_map/convert_element_type | solution.py:214
  422.4 11.1 %copy.273 = f32[37,8,8,128]{3,2,1,0:T(8,128)S(1)} copy(f32[37,8,8,128]{2,0,1,3:T(8,128)} %bitcast.528) | data formatting | bytes 2424832 | tf_op jit(solution)/shard_map/convert_element_type | solution.py:214
  440.3 63.5 %all-reduce.3 = (f32[64]{0:T(128)S(1)}, f32[64]{0:T(128)S(1)}) all-reduce(f32[64]{0:T(128)S(1)} %get-tuple-element.39, f32[64]{0:T(128)S(1)} %get-tuple-element.38), channel_id=1, replica_groups=mesh['row'=8,'col'=16] {'row','col'}, use_global_device_ids=true, to_apply=%region_11.12 | all-reduce | flops 128 | bytes 1024 | tf_op jit(solution)/shard_map/psum | solution.py:96
  540.1 5.2 copy.259
  548.4 5.6 all-to-all-start
  570.2 8.1 collective-permute-done.11
  578.3 7.2 collective-permute-done.10
  596.7 65.8 %all-reduce.2 = (f32[64]{0:T(128)S(1)}, f32[64]{0:T(128)S(1)}, f32[37,64]{1,0:T(8,128)S(1)}, f32[37]{0:T(128)S(1)}) all-reduce(f32[64]{0:T(128)S(1)} %get-tuple-element.37, f32[64]{0:T(128)S(1)} %get-tuple-element.36, f32[37,64]{1,0:T(8,128)S(1)} %convolution_bitcast_fusion.23, ...), channel_id=1, replica_groups=mesh['row'=8,'col'=16] {'row','col'}, use_global_device_ids=true, to_apply=%region_15.16 | all-reduce | flops 2533 | bytes 20264 | tf_op jit(solution)/shard_map/psum | solution.py:96
  708.6 125.4 %all-reduce.7.cloned.1.call-done = (f32[9,64,64]{2,1,0:T(8,128)}, f32[9,64,64]{2,1,0:T(8,128)}) async-done(((f32[9,64,64]{2,1,0:T(8,128)}, f32[9,64,64]{2,1,0:T(8,128)}), (f32[9,64,64]{2,1,0:T(8,128)}, f32[9,64,64]{2,1,0:T(8,128)})) %all-reduce.7.cloned.1.call-update) | async-done | bytes 294928 | tf_op jit(solution)/shard_map/psum | solution.py:241
  853.1 7.4 all-to-all-start.1
  866.5 17.9 %all-to-all-done.1 = f32[1024,1,296]{2,1,0:T(1,128)} async-done(((f32[1024,1,296]{2,1,0:T(1,128)}), f32[1024,1,296]{2,1,0:T(1,128)}, u32[]{:S(2)}, u32[]{:S(2)}) %all-to-all-start.1) | async-done | bytes 1212448 | tf_op jit(solution)/shard_map/all_to_all | solution.py:172
  887.4 5.5 all-to-all-start.2
  899.0 15.5 %all-to-all-done.2 = f32[8,16,8,296]{3,2,0,1:T(8,128)} async-done(((f32[8,16,8,296]{3,2,0,1:T(8,128)}), f32[8,16,8,296]{3,2,0,1:T(8,128)}, u32[]{:S(2)}, u32[]{:S(2)}) %all-to-all-start.2) | async-done | bytes 1212448 | tf_op jit(solution)/shard_map/all_to_all | solution.py:179
  914.5 12.2 %reshape.301 = f32[128,8,37,8]{3,2,1,0:T(8,128)} reshape(f32[16,8,1,8,296]{4,3,1,0,2:T(8,128)} %bitcast.32) | data formatting | bytes 2424832 | tf_op jit(solution)/shard_map/reshape | solution.py:124
  926.6 11.2 %copy.265 = f32[37,8,8,128]{3,2,1,0:T(8,128)S(1)} copy(f32[37,8,8,128]{2,0,1,3:T(8,128)} %bitcast.529) | data formatting | bytes 2424832 | tf_op jit(solution)/shard_map/transpose | solution.py:124
  (277 shorter events, 256.0 us)
Async XLA Ops:
  7.2 428.6 %copy-start = (bf16[37,64]{1,0:T(8,128)(2,1)S(1)}, bf16[37,64]{1,0:T(8,128)(2,1)}, u32[]{:S(2)}) copy-start(bf16[37,64]{1,0:T(8,128)(2,1)} %param.9) | copy-start | bytes 14212
  10.3 22.1 %collective-permute-start.1 = (bf16[64,64,16]{1,2,0:T(8,128)(2,1)}, bf16[64,64,16]{1,2,0:T(8,128)(2,1)}, u32[]{:S(2)}, u32[]{:S(2)}) collective-permute-start(bf16[64,64,16]{1,2,0:T(8,128)(2,1)} %copy.320), channel_id=1, source_target_pairs={{16,0},{32,16},{48,32},{64,48},{80,64},{96,80},{112,96},{17,1},{33... | collective-permute-start | bytes 393224 | tf_op jit(solution)/shard_map/ppermute | solution.py:18
  12.6 17.0 %collective-permute-start = (bf16[64,64,16]{1,2,0:T(8,128)(2,1)}, bf16[64,64,16]{1,2,0:T(8,128)(2,1)}, u32[]{:S(2)}, u32[]{:S(2)}) collective-permute-start(bf16[64,64,16]{1,2,0:T(8,128)(2,1)} %copy.319), channel_id=1, source_target_pairs={{0,16},{16,32},{32,48},{48,64},{64,80},{80,96},{96,112},{1,17},{17... | collective-permute-start | bytes 393224 | tf_op jit(solution)/shard_map/ppermute | solution.py:15
  21.1 205.4 %all-to-all-start.3 = ((bf16[16,64,296]{2,1,0:T(8,128)(2,1)}), bf16[16,64,296]{2,1,0:T(8,128)(2,1)}, u32[]{:S(2)}, u32[]{:S(2)}) async-start(bf16[16,64,296]{2,1,0:T(8,128)(2,1)} %copy.268), calls=%async_computation.3 | async-start | bytes 1572864 | tf_op jit(solution)/shard_map/all_to_all | solution.py:132
  35.8 9.7 %collective-permute-start.2 = (bf16[64,16,160]{2,0,1:T(8,128)(2,1)S(1)}, bf16[64,16,160]{2,0,1:T(8,128)(2,1)S(1)}, u32[]{:S(2)}, u32[]{:S(2)}) collective-permute-start(bf16[64,16,160]{2,0,1:T(8,128)(2,1)S(1)} %get-tuple-element.66), channel_id=1, source_target_pairs={{0,1},{1,2},{2,3},{3,4},{4,5},{5,6},{6,7},{7,8},{8,9},{9,10},{10,1... | collective-permute-start | bytes 983048 | tf_op jit(solution)/shard_map/ppermute | solution.py:15
  39.3 13.3 %collective-permute-start.3 = (bf16[64,16,160]{2,0,1:T(8,128)(2,1)S(1)}, bf16[64,16,160]{2,0,1:T(8,128)(2,1)S(1)}, u32[]{:S(2)}, u32[]{:S(2)}) collective-permute-start(bf16[64,16,160]{2,0,1:T(8,128)(2,1)S(1)} %get-tuple-element.67), channel_id=1, source_target_pairs={{1,0},{2,1},{3,2},{4,3},{5,4},{6,5},{7,6},{8,7},{9,8},{10,9},{11,1... | collective-permute-start | bytes 983048 | tf_op jit(solution)/shard_map/ppermute | solution.py:18
  199.7 7.3 collective-permute-start.4
  205.6 9.0 collective-permute-start.5
  220.7 27.0 %collective-permute-start.7 = (bf16[64,16,160]{2,0,1:T(8,128)(2,1)}, bf16[64,16,160]{2,0,1:T(8,128)(2,1)}, u32[]{:S(2)}, u32[]{:S(2)}) collective-permute-start(bf16[64,16,160]{2,0,1:T(8,128)(2,1)} %get-tuple-element.62), channel_id=1, source_target_pairs={{1,0},{2,1},{3,2},{4,3},{5,4},{6,5},{7,6},{8,7},{9,8},{10,9},{11,1... | collective-permute-start | bytes 983048 | tf_op jit(solution)/shard_map/ppermute | solution.py:18
  224.6 23.2 %collective-permute-start.6 = (bf16[64,16,160]{2,0,1:T(8,128)(2,1)}, bf16[64,16,160]{2,0,1:T(8,128)(2,1)}, u32[]{:S(2)}, u32[]{:S(2)}) collective-permute-start(bf16[64,16,160]{2,0,1:T(8,128)(2,1)} %get-tuple-element.63), channel_id=1, source_target_pairs={{0,1},{1,2},{2,3},{3,4},{4,5},{5,6},{6,7},{7,8},{8,9},{9,10},{10,1... | collective-permute-start | bytes 983048 | tf_op jit(solution)/shard_map/ppermute | solution.py:15
  233.5 94.8 %all-to-all-start.4 = ((bf16[128,2,1184]{2,1,0:T(2,128)(2,1)}), bf16[128,2,1184]{2,1,0:T(2,128)(2,1)}, u32[]{:S(2)}, u32[]{:S(2)}) async-start(bf16[128,2,1184]{2,1,0:T(2,128)(2,1)} %reshape.303), calls=%async_computation.4 | async-start | bytes 1310720 | tf_op jit(solution)/shard_map/all_to_all | solution.py:139
  337.1 71.8 %all-to-all-start.5 = ((bf16[8,16,8,296]{3,2,0,1:T(8,128)(2,1)}), bf16[8,16,8,296]{3,2,0,1:T(8,128)(2,1)S(1)}, u32[]{:S(2)}, u32[]{:S(2)}) async-start(bf16[8,16,8,296]{3,2,0,1:T(8,128)(2,1)} %copy.271), calls=%async_computation.5 | async-start | bytes 1572864 | tf_op jit(solution)/shard_map/all_to_all | solution.py:146
  524.3 33.3 %collective-permute-start.9 = (bf16[64,64,16]{1,2,0:T(8,128)(2,1)}, bf16[64,64,16]{1,2,0:T(8,128)(2,1)}, u32[]{:S(2)}, u32[]{:S(2)}) collective-permute-start(bf16[64,64,16]{1,2,0:T(8,128)(2,1)} %copy.276), channel_id=1, source_target_pairs={{16,0},{32,16},{48,32},{64,48},{80,64},{96,80},{112,96},{17,1},{33... | collective-permute-start | bytes 393224 | tf_op jit(solution)/shard_map/ppermute | solution.py:18
  525.6 28.6 %collective-permute-start.8 = (bf16[64,64,16]{1,2,0:T(8,128)(2,1)}, bf16[64,64,16]{1,2,0:T(8,128)(2,1)}, u32[]{:S(2)}, u32[]{:S(2)}) collective-permute-start(bf16[64,64,16]{1,2,0:T(8,128)(2,1)} %copy.275), channel_id=1, source_target_pairs={{0,16},{16,32},{32,48},{48,64},{64,80},{80,96},{96,112},{1,17},{17... | collective-permute-start | bytes 393224 | tf_op jit(solution)/shard_map/ppermute | solution.py:15
  548.4 300.5 %all-to-all-start = ((f32[16,64,296]{2,1,0:T(8,128)}), f32[16,64,296]{2,1,0:T(8,128)}, u32[]{:S(2)}, u32[]{:S(2)}) async-start(f32[16,64,296]{2,1,0:T(8,128)} %copy.260), calls=%async_computation | async-start | bytes 3145728 | tf_op jit(solution)/shard_map/all_to_all | solution.py:165
  554.0 280.0 %all-reduce.7.cloned.1.call-start = ((), (), s32[]{:S(2)}) async-start(), calls=%async_computation.6 | async-start | bytes 1179648 | tf_op jit(solution)/shard_map/psum | solution.py:241
  563.0 15.3 %collective-permute-start.11 = (bf16[64,16,160]{2,0,1:T(8,128)(2,1)S(1)}, bf16[64,16,160]{2,0,1:T(8,128)(2,1)S(1)}, u32[]{:S(2)}, u32[]{:S(2)}) collective-permute-start(bf16[64,16,160]{2,0,1:T(8,128)(2,1)S(1)} %get-tuple-element.58), channel_id=1, source_target_pairs={{0,1},{1,2},{2,3},{3,4},{4,5},{5,6},{6,7},{7,8},{8,9},{9,10},{10,1... | collective-permute-start | bytes 983048 | tf_op jit(solution)/shard_map/ppermute | solution.py:15
  566.5 18.9 %collective-permute-start.10 = (bf16[64,16,160]{2,0,1:T(8,128)(2,1)S(1)}, bf16[64,16,160]{2,0,1:T(8,128)(2,1)S(1)}, u32[]{:S(2)}, u32[]{:S(2)}) collective-permute-start(bf16[64,16,160]{2,0,1:T(8,128)(2,1)S(1)} %get-tuple-element.59), channel_id=1, source_target_pairs={{1,0},{2,1},{3,2},{4,3},{5,4},{6,5},{7,6},{8,7},{9,8},{10,9},{11,1... | collective-permute-start | bytes 983048 | tf_op jit(solution)/shard_map/ppermute | solution.py:18
  679.8 13.4 %collective-permute-start.13 = (bf16[64,64,16]{1,2,0:T(8,128)(2,1)}, bf16[64,64,16]{1,2,0:T(8,128)(2,1)}, u32[]{:S(2)}, u32[]{:S(2)}) collective-permute-start(bf16[64,64,16]{1,2,0:T(8,128)(2,1)} %copy.292), channel_id=1, source_target_pairs={{16,0},{32,16},{48,32},{64,48},{80,64},{96,80},{112,96},{17,1},{33... | collective-permute-start | bytes 393224 | tf_op jit(solution)/shard_map/ppermute | solution.py:18
  681.1 8.8 collective-permute-start.12
  699.5 137.9 %collective-permute-start.15 = (bf16[64,16,160]{2,0,1:T(8,128)(2,1)}, bf16[64,16,160]{2,0,1:T(8,128)(2,1)}, u32[]{:S(2)}, u32[]{:S(2)}) collective-permute-start(bf16[64,16,160]{2,0,1:T(8,128)(2,1)} %get-tuple-element.54), channel_id=1, source_target_pairs={{0,1},{1,2},{2,3},{3,4},{4,5},{5,6},{6,7},{7,8},{8,9},{9,10},{10,1... | collective-permute-start | bytes 983048 | tf_op jit(solution)/shard_map/ppermute | solution.py:15
  704.1 133.3 %collective-permute-start.14 = (bf16[64,16,160]{2,0,1:T(8,128)(2,1)}, bf16[64,16,160]{2,0,1:T(8,128)(2,1)}, u32[]{:S(2)}, u32[]{:S(2)}) collective-permute-start(bf16[64,16,160]{2,0,1:T(8,128)(2,1)} %get-tuple-element.55), channel_id=1, source_target_pairs={{1,0},{2,1},{3,2},{4,3},{5,4},{6,5},{7,6},{8,7},{9,8},{10,9},{11,1... | collective-permute-start | bytes 983048 | tf_op jit(solution)/shard_map/ppermute | solution.py:18
  853.1 31.4 %all-to-all-start.1 = ((f32[1024,1,296]{2,1,0:T(1,128)}), f32[1024,1,296]{2,1,0:T(1,128)}, u32[]{:S(2)}, u32[]{:S(2)}) async-start(f32[1024,1,296]{2,1,0:T(1,128)} %copy.261), calls=%async_computation.1 | async-start | bytes 3145728 | tf_op jit(solution)/shard_map/all_to_all | solution.py:172
  887.4 27.1 %all-to-all-start.2 = ((f32[8,16,8,296]{3,2,0,1:T(8,128)}), f32[8,16,8,296]{3,2,0,1:T(8,128)}, u32[]{:S(2)}, u32[]{:S(2)}) async-start(f32[8,16,8,296]{3,2,0,1:T(8,128)} %copy.263), calls=%async_computation.2 | async-start | bytes 3145728 | tf_op jit(solution)/shard_map/all_to_all | solution.py:179
  (48 other events, 293.4 us)
Sparse Core Ops, SparseCore 0:
  686.4 147.6 all-reduce.6
